TPU v7x, 256 devices: a whole 4x4x8 slice. The times are simulated.
256 devices in a mesh: rhs: 32 (over x, z_lo, y), node: 8 (over z_hi, core).
Axes of the slice: x: 4, y: 4, z: 8 (z_hi: 4, z_lo: 2; z = z_hi * 2 + z_lo), core: 2. Of those that a mesh axis runs over, the one named last changes fastest.
Arguments:
- right_side: float32 [8192, 8192], P('node', 'rhs'), may hold values from -6 to 6
- diag_inv: float32 [32, 256, 256], P('node', 'rhs'), may hold values from -1 to 1
- lower: float32 [32, 256, 256], P('node', 'rhs'), may hold values from -0.4375 to 0.4375
- factor_pattern: int32 [32, 4, 4], P('node'), may hold values 0 or 1
- jacobian: float32 [32, 256, 768], P('node', 'rhs'), may hold values from -0.078125 to 0.078125
- jacobian_pattern: int32 [32, 4, 12], P('node'), may hold values 0 or 1
Outputs:
- solution: float32 [8192, 8192], P('node', 'rhs')
- residual: float32 [8192, 8192], P('node', 'rhs')
All inputs are finite; a program needn't handle non-finite values. No bound on the sum of `factor_pattern` or of `jacobian_pattern` on one device may be relied on, other than what follows from the above.
Results may differ from a plain program's by a relative error of at most 0.00021.
Values sent between devices are 32-bit elements; how exact they have to be, the bound alone decides.
A program may use at most 64 MiB of HBM per device.

v0:
```python
import jax
import jax.numpy as jnp
from jax import lax
from jax.sharding import PartitionSpec as P

HIGHEST_PREC = lax.Precision.HIGHEST
TRANSPOSED = (((0,), (0,)), ((), ()))


def shifted(value, axis, steps):
    count = lax.axis_size(axis)
    initial, last = (max(0, -steps), min(count, count - steps))
    return lax.ppermute(value, axis, [(source, source + steps) for source in range(initial, last)])


def extended(cells, sides, width):
    for axis, dim in sides:
        count = lax.axis_size(axis)
        ends = count - 1
        head = lax.slice_in_dim(cells, 0, width, axis=dim)
        tail = lax.slice_in_dim(cells, cells.shape[dim] - width, cells.shape[dim], axis=dim)
        cells = jnp.concatenate(
            [
                lax.ppermute(tail, axis, [(i, (i + 1) % count) for i in range(ends)]),
                cells,
                lax.ppermute(head, axis, [((i + 1) % count, i) for i in range(ends)]),
            ],
            axis=dim,
        )
    return cells


def apply_pattern(blocks, pattern):
    supers, row_count, col_count = blocks.shape
    block_size = row_count // pattern.shape[1]
    shaped = blocks.reshape(supers, pattern.shape[1], block_size, pattern.shape[2], block_size)
    weights = pattern.astype(jnp.float32)[:, :, None, :, None]
    return (shaped * weights).reshape(supers, row_count, col_count)


def sweep_down(inverse, masked, rhs_blocks, incoming):

    def advance(previous, inputs):
        inv_block, low_block, rhs_block = inputs
        coupled = jnp.dot(low_block, previous, precision=HIGHEST_PREC)
        solved = jnp.dot(inv_block, rhs_block - coupled, precision=HIGHEST_PREC)
        return (solved, solved)

    outgoing, values = lax.scan(advance, incoming, (inverse, masked, rhs_blocks))
    return (values, outgoing)


def sweep_up(inverse, masked, forward_blocks, incoming):

    def advance(entering, inputs):
        inv_block, low_block, forward_block = inputs
        solved = lax.dot_general(
            inv_block, forward_block - entering, TRANSPOSED, precision=HIGHEST_PREC
        )
        passed = lax.dot_general(low_block, solved, TRANSPOSED, precision=HIGHEST_PREC)
        return (passed, solved)

    outgoing, values = lax.scan(advance, incoming, (inverse, masked, forward_blocks), reverse=True)
    return (values, outgoing)


def jacobian_product(portion, pattern, windows):
    supers, row_count, col_count = portion.shape
    block_count = pattern.shape[1]
    block_size = col_count // pattern.shape[2]
    row_ids = lax.iota(jnp.int32, row_count)
    onehot = (row_ids[:, None] // block_size == lax.iota(jnp.int32, block_count)[None, :]).astype(
        jnp.float32
    )
    weights = jnp.einsum("ra,sac->src", onehot, pattern.astype(jnp.float32))
    shaped = portion.reshape(supers, row_count, pattern.shape[2], block_size)
    masked = (shaped * weights[:, :, :, None]).reshape(supers, row_count, col_count)
    return jnp.einsum("sij,sjr->sir", masked, windows, precision=HIGHEST_PREC)


def on_device(right_side, diag_inv, lower, factor_pattern, jacobian, jacobian_pattern):
    supers = diag_inv.shape[0]
    panel_rows = diag_inv.shape[2]
    columns = right_side.shape[1]
    rhs_blocks = right_side.reshape(supers, panel_rows, columns)
    inverse, lower_all = (
        lax.all_gather(diag_inv, "rhs", axis=1, tiled=True),
        lax.all_gather(lower, "rhs", axis=1, tiled=True),
    )
    masked = apply_pattern(lower_all, factor_pattern)
    zero_state = jnp.zeros((panel_rows, columns), jnp.float32)
    rounds = lax.axis_size("node")

    def relay_down(round_index, incoming):
        unused, outgoing = sweep_down(inverse, masked, rhs_blocks, incoming)
        return shifted(outgoing, "node", 1)

    incoming = lax.fori_loop(0, rounds - 1, relay_down, zero_state)
    forward, unused = sweep_down(inverse, masked, rhs_blocks, incoming)

    def relay_up(round_index, incoming):
        unused, outgoing = sweep_up(inverse, masked, forward, incoming)
        return shifted(outgoing, "node", -1)

    incoming = lax.fori_loop(0, rounds - 1, relay_up, zero_state)
    solution, unused = sweep_up(inverse, masked, forward, incoming)
    span = supers * panel_rows
    flattened = solution.reshape(span, columns)
    padded = extended(flattened, (("node", 0),), panel_rows)
    before = padded[:span].reshape(supers, panel_rows, columns)
    after = padded[2 * panel_rows :].reshape(supers, panel_rows, columns)
    windows = jnp.concatenate([before, solution, after], axis=1)
    product = jacobian_product(
        lax.all_gather(jacobian, "rhs", axis=1, tiled=True), jacobian_pattern, windows
    )
    residual = rhs_blocks - product
    return (flattened, residual.reshape(span, columns))


def solution(mesh):
    in_specs = (
        P("node", "rhs"),
        P("node", "rhs", None),
        P("node", "rhs", None),
        P("node", None, None),
        P("node", "rhs", None),
        P("node", None, None),
    )
    out_specs = (P("node", "rhs"), P("node", "rhs"))
    return jax.shard_map(
        on_device, mesh=mesh, in_specs=in_specs, out_specs=out_specs, check_vma=False
    )
```

profile of v0, /device:TPU:1, one launch (start us, length us, event | category | flops | bytes accessed | tf_op | source)
XLA Modules:
  0.0 639.9 jit_solution(5976639583881987861)
XLA Ops:
  13.5 131.2 %all-gather.4.cloned.1.call-done = f32[4,256,256]{2,1,0:T(8,128)} async-done(((f32[4,8,256]{2,1,0:T(8,128)}), f32[4,256,256]{2,1,0:T(8,128)}) %all-gather.4.cloned.1.call-update) | async-done | bytes 1048592 | tf_op jit(solution)/shard_map/all_gather | solution.py:88
  146.3 153.1 %all-gather.6.cloned.1.call-done = f32[4,256,256]{2,1,0:T(8,128)} async-done(((f32[4,8,256]{2,1,0:T(8,128)}), f32[4,256,256]{2,1,0:T(8,128)}) %all-gather.6.cloned.1.call-update) | async-done | bytes 1048592 | tf_op jit(solution)/shard_map/all_gather | solution.py:87
  299.4 141.4 %while.89 = (s32[]{:T(128)}, f32[256,256]{1,0:T(8,128)S(1)}, f32[4,256,256]{2,1,0:T(8,128)}, f32[4,256,256]{2,1,0:T(8,128)S(1)}, f32[4,256,256]{2,1,0:T(8,128)S(...) while((s32[]{:T(128)}, f32[256,256]{1,0:T(8,128)S(1)}, f32[4,256,256]{2,1,0:T(8,128)}, ...), condition=%wide.region_3.4_spmd, body=%wide.region_0.3_spmd.sunk | while | flops 402718720 | bytes 3409166 | solution.py:98
  299.4 7.0 %while.94 = (s32[]{:T(128)}, f32[256,256]{1,0:T(8,128)S(1)}, f32[4,256,256]{2,1,0:T(8,128)}, f32[4,256,256]{2,1,0:T(8,128)S(1)}, f32[4,256,256]{2,1,0:T(8,128)S(1)}, /*index=5*/s32[]{:T(128)}) while((s32[]{:T(128)}, f32[256,256]{1,0:T(8,128)S(1)}, f32[4,256,256]{2,1,0:T(8,128)}, f32[4,256,256]{2,1,0:T(8,128)S(1)}, ...), condition=%wide.region_2.2_spmd, body=%wide.region_1.1_spmd.sunk | while | flops 402718720 | bytes 1836113 | solution.py:49
  306.4 27.2 %collective-permute-start.1 = (f32[256,256]{1,0:T(8,128)S(1)}, f32[256,256]{1,0:T(8,128)S(1)}, u32[]{:S(2)}, u32[]{:S(2)}) collective-permute-start(f32[256,256]{1,0:T(8,128)S(1)} %get-tuple-element.703), channel_id=1, source_target_pairs={{0,1},{1,2},{2,3},{3,4},{4,5},{5,6},{6,7},{8,9},{9,10},{10,11},{11... | collective-permute-start | bytes 786440 | tf_op jit(solution)/shard_map/while/body/eval_jaxpr/ppermute | solution.py:13
  333.7 4.3 collective-permute-done.1
  338.1 7.0 %while.94 = (s32[]{:T(128)}, f32[256,256]{1,0:T(8,128)S(1)}, f32[4,256,256]{2,1,0:T(8,128)}, f32[4,256,256]{2,1,0:T(8,128)S(1)}, f32[4,256,256]{2,1,0:T(8,128)S(1)}, /*index=5*/s32[]{:T(128)}) while((s32[]{:T(128)}, f32[256,256]{1,0:T(8,128)S(1)}, f32[4,256,256]{2,1,0:T(8,128)}, f32[4,256,256]{2,1,0:T(8,128)S(1)}, ...), condition=%wide.region_2.2_spmd, body=%wide.region_1.1_spmd.sunk | while | flops 402718720 | bytes 1836113 | solution.py:49
  345.1 5.3 collective-permute-start.1
  350.3 4.5 collective-permute-done.1
  354.9 7.0 %while.94 = (s32[]{:T(128)}, f32[256,256]{1,0:T(8,128)S(1)}, f32[4,256,256]{2,1,0:T(8,128)}, f32[4,256,256]{2,1,0:T(8,128)S(1)}, f32[4,256,256]{2,1,0:T(8,128)S(1)}, /*index=5*/s32[]{:T(128)}) while((s32[]{:T(128)}, f32[256,256]{1,0:T(8,128)S(1)}, f32[4,256,256]{2,1,0:T(8,128)}, f32[4,256,256]{2,1,0:T(8,128)S(1)}, ...), condition=%wide.region_2.2_spmd, body=%wide.region_1.1_spmd.sunk | while | flops 402718720 | bytes 1836113 | solution.py:49
  361.8 5.3 collective-permute-start.1
  367.1 3.9 collective-permute-done.1
  371.0 7.0 %while.94 = (s32[]{:T(128)}, f32[256,256]{1,0:T(8,128)S(1)}, f32[4,256,256]{2,1,0:T(8,128)}, f32[4,256,256]{2,1,0:T(8,128)S(1)}, f32[4,256,256]{2,1,0:T(8,128)S(1)}, /*index=5*/s32[]{:T(128)}) while((s32[]{:T(128)}, f32[256,256]{1,0:T(8,128)S(1)}, f32[4,256,256]{2,1,0:T(8,128)}, f32[4,256,256]{2,1,0:T(8,128)S(1)}, ...), condition=%wide.region_2.2_spmd, body=%wide.region_1.1_spmd.sunk | while | flops 402718720 | bytes 1836113 | solution.py:49
  378.0 5.4 collective-permute-start.1
  383.5 5.3 collective-permute-done.1
  388.8 7.0 %while.94 = (s32[]{:T(128)}, f32[256,256]{1,0:T(8,128)S(1)}, f32[4,256,256]{2,1,0:T(8,128)}, f32[4,256,256]{2,1,0:T(8,128)S(1)}, f32[4,256,256]{2,1,0:T(8,128)S(1)}, /*index=5*/s32[]{:T(128)}) while((s32[]{:T(128)}, f32[256,256]{1,0:T(8,128)S(1)}, f32[4,256,256]{2,1,0:T(8,128)}, f32[4,256,256]{2,1,0:T(8,128)S(1)}, ...), condition=%wide.region_2.2_spmd, body=%wide.region_1.1_spmd.sunk | while | flops 402718720 | bytes 1836113 | solution.py:49
  395.8 5.3 collective-permute-start.1
  401.0 3.8 collective-permute-done.1
  404.9 7.0 %while.94 = (s32[]{:T(128)}, f32[256,256]{1,0:T(8,128)S(1)}, f32[4,256,256]{2,1,0:T(8,128)}, f32[4,256,256]{2,1,0:T(8,128)S(1)}, f32[4,256,256]{2,1,0:T(8,128)S(1)}, /*index=5*/s32[]{:T(128)}) while((s32[]{:T(128)}, f32[256,256]{1,0:T(8,128)S(1)}, f32[4,256,256]{2,1,0:T(8,128)}, f32[4,256,256]{2,1,0:T(8,128)S(1)}, ...), condition=%wide.region_2.2_spmd, body=%wide.region_1.1_spmd.sunk | while | flops 402718720 | bytes 1836113 | solution.py:49
  411.9 5.3 collective-permute-start.1
  417.2 4.3 collective-permute-done.1
  421.6 7.0 %while.94 = (s32[]{:T(128)}, f32[256,256]{1,0:T(8,128)S(1)}, f32[4,256,256]{2,1,0:T(8,128)}, f32[4,256,256]{2,1,0:T(8,128)S(1)}, f32[4,256,256]{2,1,0:T(8,128)S(1)}, /*index=5*/s32[]{:T(128)}) while((s32[]{:T(128)}, f32[256,256]{1,0:T(8,128)S(1)}, f32[4,256,256]{2,1,0:T(8,128)}, f32[4,256,256]{2,1,0:T(8,128)S(1)}, ...), condition=%wide.region_2.2_spmd, body=%wide.region_1.1_spmd.sunk | while | flops 402718720 | bytes 1836113 | solution.py:49
  428.6 7.2 %collective-permute-start.1 = (f32[256,256]{1,0:T(8,128)S(1)}, f32[256,256]{1,0:T(8,128)S(1)}, u32[]{:S(2)}, u32[]{:S(2)}) collective-permute-start(f32[256,256]{1,0:T(8,128)S(1)} %get-tuple-element.703), channel_id=1, source_target_pairs={{0,1},{1,2},{2,3},{3,4},{4,5},{5,6},{6,7},{8,9},{9,10},{10,11},{11... | collective-permute-start | bytes 786440 | tf_op jit(solution)/shard_map/while/body/eval_jaxpr/ppermute | solution.py:13
  435.8 5.0 collective-permute-done.1
  440.9 7.0 %while.90 = (s32[]{:T(128)}, f32[256,256]{1,0:T(8,128)S(1)}, f32[4,256,256]{2,1,0:T(8,128)S(1)}, f32[4,256,256]{2,1,0:T(8,128)}, f32[4,256,256]{2,1,0:T(8,128)S(1)}, /*index=5*/f32[4,256,256]{2,1,0:T(8,128)S(1)}, s32[]{:T(128)}) while((s32[]{:T(128)}, f32[256,256]{1,0:T(8,128)S(1)}, f32[4,256,256]{2,1,0:T(8,128)S(1)}, ...), condition=%wide.region_5.6_spmd, body=%wide.region_4.5_spmd.sunk | while | flops 402718720 | bytes 2099285 | solution.py:49
  447.9 138.3 %while.92 = (s32[]{:T(128)}, f32[256,256]{1,0:T(8,128)S(1)}, f32[4,256,256]{2,1,0:T(8,128)S(1)}, f32[4,256,256]{2,1,0:T(8,128)}, f32[4,256,256]{2,1,0:T(8,128)S(...) while((s32[]{:T(128)}, f32[256,256]{1,0:T(8,128)S(1)}, f32[4,256,256]{2,1,0:T(8,128)S(1)}, ...), condition=%wide.region_9.10_spmd, body=%wide.region_6.9_spmd.sunk | while | flops 402718720 | bytes 3409194 | solution.py:105
  447.9 8.7 %while.95 = (s32[]{:T(128)}, f32[256,256]{1,0:T(8,128)S(1)}, f32[4,256,256]{2,1,0:T(8,128)S(1)}, f32[4,256,256]{2,1,0:T(8,128)}, f32[4,256,256]{2,1,0:T(8,128)S(1)}, /*index=5*/s32[]{:T(128)}, s32[]{:T(128)}) while((s32[]{:T(128)}, f32[256,256]{1,0:T(8,128)S(1)}, f32[4,256,256]{2,1,0:T(8,128)S(1)}, f32[4,256,256]{2,1,0:T(8,128)}, ...), condition=%wide.region_8.8_spmd, body=%wide.region_7.7_spmd.sunk | while | flops 402718720 | bytes 1836133 | solution.py:63
  458.6 7.9 %collective-permute-done = f32[256,256]{1,0:T(8,128)} collective-permute-done((f32[256,256]{1,0:T(8,128)S(1)}, f32[256,256]{1,0:T(8,128)}, u32[]{:S(2)}, u32[]{:S(2)}) %collective-permute-start) | collective-permute-done | bytes 262176 | tf_op jit(solution)/shard_map/while/body/eval_jaxpr/ppermute | solution.py:13
  467.4 8.7 %while.95 = (s32[]{:T(128)}, f32[256,256]{1,0:T(8,128)S(1)}, f32[4,256,256]{2,1,0:T(8,128)S(1)}, f32[4,256,256]{2,1,0:T(8,128)}, f32[4,256,256]{2,1,0:T(8,128)S(1)}, /*index=5*/s32[]{:T(128)}, s32[]{:T(128)}) while((s32[]{:T(128)}, f32[256,256]{1,0:T(8,128)S(1)}, f32[4,256,256]{2,1,0:T(8,128)S(1)}, f32[4,256,256]{2,1,0:T(8,128)}, ...), condition=%wide.region_8.8_spmd, body=%wide.region_7.7_spmd.sunk | while | flops 402718720 | bytes 1836133 | solution.py:63
  478.1 8.3 %collective-permute-done = f32[256,256]{1,0:T(8,128)} collective-permute-done((f32[256,256]{1,0:T(8,128)S(1)}, f32[256,256]{1,0:T(8,128)}, u32[]{:S(2)}, u32[]{:S(2)}) %collective-permute-start) | collective-permute-done | bytes 262176 | tf_op jit(solution)/shard_map/while/body/eval_jaxpr/ppermute | solution.py:13
  487.3 8.7 %while.95 = (s32[]{:T(128)}, f32[256,256]{1,0:T(8,128)S(1)}, f32[4,256,256]{2,1,0:T(8,128)S(1)}, f32[4,256,256]{2,1,0:T(8,128)}, f32[4,256,256]{2,1,0:T(8,128)S(1)}, /*index=5*/s32[]{:T(128)}, s32[]{:T(128)}) while((s32[]{:T(128)}, f32[256,256]{1,0:T(8,128)S(1)}, f32[4,256,256]{2,1,0:T(8,128)S(1)}, f32[4,256,256]{2,1,0:T(8,128)}, ...), condition=%wide.region_8.8_spmd, body=%wide.region_7.7_spmd.sunk | while | flops 402718720 | bytes 1836133 | solution.py:63
  497.9 9.0 %collective-permute-done = f32[256,256]{1,0:T(8,128)} collective-permute-done((f32[256,256]{1,0:T(8,128)S(1)}, f32[256,256]{1,0:T(8,128)}, u32[]{:S(2)}, u32[]{:S(2)}) %collective-permute-start) | collective-permute-done | bytes 262176 | tf_op jit(solution)/shard_map/while/body/eval_jaxpr/ppermute | solution.py:13
  507.9 8.7 %while.95 = (s32[]{:T(128)}, f32[256,256]{1,0:T(8,128)S(1)}, f32[4,256,256]{2,1,0:T(8,128)S(1)}, f32[4,256,256]{2,1,0:T(8,128)}, f32[4,256,256]{2,1,0:T(8,128)S(1)}, /*index=5*/s32[]{:T(128)}, s32[]{:T(128)}) while((s32[]{:T(128)}, f32[256,256]{1,0:T(8,128)S(1)}, f32[4,256,256]{2,1,0:T(8,128)S(1)}, f32[4,256,256]{2,1,0:T(8,128)}, ...), condition=%wide.region_8.8_spmd, body=%wide.region_7.7_spmd.sunk | while | flops 402718720 | bytes 1836133 | solution.py:63
  518.5 8.0 %collective-permute-done = f32[256,256]{1,0:T(8,128)} collective-permute-done((f32[256,256]{1,0:T(8,128)S(1)}, f32[256,256]{1,0:T(8,128)}, u32[]{:S(2)}, u32[]{:S(2)}) %collective-permute-start) | collective-permute-done | bytes 262176 | tf_op jit(solution)/shard_map/while/body/eval_jaxpr/ppermute | solution.py:13
  527.5 8.7 %while.95 = (s32[]{:T(128)}, f32[256,256]{1,0:T(8,128)S(1)}, f32[4,256,256]{2,1,0:T(8,128)S(1)}, f32[4,256,256]{2,1,0:T(8,128)}, f32[4,256,256]{2,1,0:T(8,128)S(1)}, /*index=5*/s32[]{:T(128)}, s32[]{:T(128)}) while((s32[]{:T(128)}, f32[256,256]{1,0:T(8,128)S(1)}, f32[4,256,256]{2,1,0:T(8,128)S(1)}, f32[4,256,256]{2,1,0:T(8,128)}, ...), condition=%wide.region_8.8_spmd, body=%wide.region_7.7_spmd.sunk | while | flops 402718720 | bytes 1836133 | solution.py:63
  538.1 8.0 %collective-permute-done = f32[256,256]{1,0:T(8,128)} collective-permute-done((f32[256,256]{1,0:T(8,128)S(1)}, f32[256,256]{1,0:T(8,128)}, u32[]{:S(2)}, u32[]{:S(2)}) %collective-permute-start) | collective-permute-done | bytes 262176 | tf_op jit(solution)/shard_map/while/body/eval_jaxpr/ppermute | solution.py:13
  547.0 8.7 %while.95 = (s32[]{:T(128)}, f32[256,256]{1,0:T(8,128)S(1)}, f32[4,256,256]{2,1,0:T(8,128)S(1)}, f32[4,256,256]{2,1,0:T(8,128)}, f32[4,256,256]{2,1,0:T(8,128)S(1)}, /*index=5*/s32[]{:T(128)}, s32[]{:T(128)}) while((s32[]{:T(128)}, f32[256,256]{1,0:T(8,128)S(1)}, f32[4,256,256]{2,1,0:T(8,128)S(1)}, f32[4,256,256]{2,1,0:T(8,128)}, ...), condition=%wide.region_8.8_spmd, body=%wide.region_7.7_spmd.sunk | while | flops 402718720 | bytes 1836133 | solution.py:63
  557.7 8.0 %collective-permute-done = f32[256,256]{1,0:T(8,128)} collective-permute-done((f32[256,256]{1,0:T(8,128)S(1)}, f32[256,256]{1,0:T(8,128)}, u32[]{:S(2)}, u32[]{:S(2)}) %collective-permute-start) | collective-permute-done | bytes 262176 | tf_op jit(solution)/shard_map/while/body/eval_jaxpr/ppermute | solution.py:13
  566.6 8.7 %while.95 = (s32[]{:T(128)}, f32[256,256]{1,0:T(8,128)S(1)}, f32[4,256,256]{2,1,0:T(8,128)S(1)}, f32[4,256,256]{2,1,0:T(8,128)}, f32[4,256,256]{2,1,0:T(8,128)S(1)}, /*index=5*/s32[]{:T(128)}, s32[]{:T(128)}) while((s32[]{:T(128)}, f32[256,256]{1,0:T(8,128)S(1)}, f32[4,256,256]{2,1,0:T(8,128)S(1)}, f32[4,256,256]{2,1,0:T(8,128)}, ...), condition=%wide.region_8.8_spmd, body=%wide.region_7.7_spmd.sunk | while | flops 402718720 | bytes 1836133 | solution.py:63
  577.3 8.0 %collective-permute-done = f32[256,256]{1,0:T(8,128)} collective-permute-done((f32[256,256]{1,0:T(8,128)S(1)}, f32[256,256]{1,0:T(8,128)}, u32[]{:S(2)}, u32[]{:S(2)}) %collective-permute-start) | collective-permute-done | bytes 262176 | tf_op jit(solution)/shard_map/while/body/eval_jaxpr/ppermute | solution.py:13
  587.3 11.5 %while.93 = (s32[]{:T(128)}, f32[256,256]{1,0:T(8,128)S(1)}, f32[4,256,256]{2,1,0:T(8,128)}, f32[4,256,256]{2,1,0:T(8,128)S(1)}, f32[4,256,256]{2,1,0:T(8,128)},...) while((s32[]{:T(128)}, f32[256,256]{1,0:T(8,128)S(1)}, f32[4,256,256]{2,1,0:T(8,128)}, ...), condition=%wide.region_11.12_spmd, body=%wide.region_10.11_spmd.sunk | while | flops 402718720 | bytes 2098797 | solution.py:63
  587.3 2.3 bitcast_dynamic-update-slice_fusion.5
  590.2 2.3 bitcast_dynamic-update-slice_fusion.5
  593.0 2.3 bitcast_dynamic-update-slice_fusion.5
  599.9 5.7 collective-permute-start.2
  608.9 9.5 %collective-permute-done.3 = f32[256,256]{1,0:T(8,128)S(1)} collective-permute-done((f32[256,256]{1,0:T(8,128)S(1)}, f32[256,256]{1,0:T(8,128)S(1)}, u32[]{:S(2)}, u32[]{:S(2)}) %collective-permute-start.3) | collective-permute-done | bytes 262176 | tf_op jit(solution)/shard_map/ppermute | solution.py:26
  620.0 4.9 copy.12
  627.1 6.4 fusion.38
  (175 shorter events, 157.1 us)
Async XLA Ops:
  7.2 137.5 %all-gather.4.cloned.1.call-start = ((), (), s32[]{:S(2)}) async-start(), calls=%async_computation | async-start | bytes 1081344 | tf_op jit(solution)/shard_map/all_gather | solution.py:88
  7.9 291.5 %all-gather.6.cloned.1.call-start = ((), (), s32[]{:S(2)}) async-start(), calls=%async_computation.1 | async-start | bytes 1081344 | tf_op jit(solution)/shard_map/all_gather | solution.py:87
  8.6 611.3 %all-gather.8.cloned.1.call-start = ((), (), s32[]{:S(2)}) async-start(), calls=%async_computation.2 | async-start | bytes 3244032 | tf_op jit(solution)/shard_map/all_gather | solution.py:114
  11.3 288.1 %copy-start = (f32[1024,256]{1,0:T(8,128)S(1)}, f32[1024,256]{1,0:T(8,128)}, u32[]{:S(2)}) copy-start(f32[1024,256]{1,0:T(8,128)} %param.18) | copy-start | bytes 3145732
  306.4 31.6 %collective-permute-start.1 = (f32[256,256]{1,0:T(8,128)S(1)}, f32[256,256]{1,0:T(8,128)S(1)}, u32[]{:S(2)}, u32[]{:S(2)}) collective-permute-start(f32[256,256]{1,0:T(8,128)S(1)} %get-tuple-element.703), channel_id=1, source_target_pairs={{0,1},{1,2},{2,3},{3,4},{4,5},{5,6},{6,7},{8,9},{9,10},{10,11},{11... | collective-permute-start | bytes 786440 | tf_op jit(solution)/shard_map/while/body/eval_jaxpr/ppermute | solution.py:13
  345.1 9.8 %collective-permute-start.1 = (f32[256,256]{1,0:T(8,128)S(1)}, f32[256,256]{1,0:T(8,128)S(1)}, u32[]{:S(2)}, u32[]{:S(2)}) collective-permute-start(f32[256,256]{1,0:T(8,128)S(1)} %get-tuple-element.703), channel_id=1, source_target_pairs={{0,1},{1,2},{2,3},{3,4},{4,5},{5,6},{6,7},{8,9},{9,10},{10,11},{11... | collective-permute-start | bytes 786440 | tf_op jit(solution)/shard_map/while/body/eval_jaxpr/ppermute | solution.py:13
  361.8 9.2 %collective-permute-start.1 = (f32[256,256]{1,0:T(8,128)S(1)}, f32[256,256]{1,0:T(8,128)S(1)}, u32[]{:S(2)}, u32[]{:S(2)}) collective-permute-start(f32[256,256]{1,0:T(8,128)S(1)} %get-tuple-element.703), channel_id=1, source_target_pairs={{0,1},{1,2},{2,3},{3,4},{4,5},{5,6},{6,7},{8,9},{9,10},{10,11},{11... | collective-permute-start | bytes 786440 | tf_op jit(solution)/shard_map/while/body/eval_jaxpr/ppermute | solution.py:13
  378.0 10.7 %collective-permute-start.1 = (f32[256,256]{1,0:T(8,128)S(1)}, f32[256,256]{1,0:T(8,128)S(1)}, u32[]{:S(2)}, u32[]{:S(2)}) collective-permute-start(f32[256,256]{1,0:T(8,128)S(1)} %get-tuple-element.703), channel_id=1, source_target_pairs={{0,1},{1,2},{2,3},{3,4},{4,5},{5,6},{6,7},{8,9},{9,10},{10,11},{11... | collective-permute-start | bytes 786440 | tf_op jit(solution)/shard_map/while/body/eval_jaxpr/ppermute | solution.py:13
  395.8 9.1 %collective-permute-start.1 = (f32[256,256]{1,0:T(8,128)S(1)}, f32[256,256]{1,0:T(8,128)S(1)}, u32[]{:S(2)}, u32[]{:S(2)}) collective-permute-start(f32[256,256]{1,0:T(8,128)S(1)} %get-tuple-element.703), channel_id=1, source_target_pairs={{0,1},{1,2},{2,3},{3,4},{4,5},{5,6},{6,7},{8,9},{9,10},{10,11},{11... | collective-permute-start | bytes 786440 | tf_op jit(solution)/shard_map/while/body/eval_jaxpr/ppermute | solution.py:13
  411.9 9.6 %collective-permute-start.1 = (f32[256,256]{1,0:T(8,128)S(1)}, f32[256,256]{1,0:T(8,128)S(1)}, u32[]{:S(2)}, u32[]{:S(2)}) collective-permute-start(f32[256,256]{1,0:T(8,128)S(1)} %get-tuple-element.703), channel_id=1, source_target_pairs={{0,1},{1,2},{2,3},{3,4},{4,5},{5,6},{6,7},{8,9},{9,10},{10,11},{11... | collective-permute-start | bytes 786440 | tf_op jit(solution)/shard_map/while/body/eval_jaxpr/ppermute | solution.py:13
  428.6 12.2 %collective-permute-start.1 = (f32[256,256]{1,0:T(8,128)S(1)}, f32[256,256]{1,0:T(8,128)S(1)}, u32[]{:S(2)}, u32[]{:S(2)}) collective-permute-start(f32[256,256]{1,0:T(8,128)S(1)} %get-tuple-element.703), channel_id=1, source_target_pairs={{0,1},{1,2},{2,3},{3,4},{4,5},{5,6},{6,7},{8,9},{9,10},{10,11},{11... | collective-permute-start | bytes 786440 | tf_op jit(solution)/shard_map/while/body/eval_jaxpr/ppermute | solution.py:13
  456.7 9.8 %collective-permute-start = (f32[256,256]{1,0:T(8,128)S(1)}, f32[256,256]{1,0:T(8,128)}, u32[]{:S(2)}, u32[]{:S(2)}) collective-permute-start(f32[256,256]{1,0:T(8,128)S(1)} %get-tuple-element.718), channel_id=1, source_target_pairs={{1,0},{2,1},{3,2},{4,3},{5,4},{6,5},{7,6},{9,8},{10,9},{11,10},{12... | collective-permute-start | bytes 786440 | tf_op jit(solution)/shard_map/while/body/eval_jaxpr/ppermute | solution.py:13
  476.2 10.2 %collective-permute-start = (f32[256,256]{1,0:T(8,128)S(1)}, f32[256,256]{1,0:T(8,128)}, u32[]{:S(2)}, u32[]{:S(2)}) collective-permute-start(f32[256,256]{1,0:T(8,128)S(1)} %get-tuple-element.718), channel_id=1, source_target_pairs={{1,0},{2,1},{3,2},{4,3},{5,4},{6,5},{7,6},{9,8},{10,9},{11,10},{12... | collective-permute-start | bytes 786440 | tf_op jit(solution)/shard_map/while/body/eval_jaxpr/ppermute | solution.py:13
  496.0 10.9 %collective-permute-start = (f32[256,256]{1,0:T(8,128)S(1)}, f32[256,256]{1,0:T(8,128)}, u32[]{:S(2)}, u32[]{:S(2)}) collective-permute-start(f32[256,256]{1,0:T(8,128)S(1)} %get-tuple-element.718), channel_id=1, source_target_pairs={{1,0},{2,1},{3,2},{4,3},{5,4},{6,5},{7,6},{9,8},{10,9},{11,10},{12... | collective-permute-start | bytes 786440 | tf_op jit(solution)/shard_map/while/body/eval_jaxpr/ppermute | solution.py:13
  516.6 9.9 %collective-permute-start = (f32[256,256]{1,0:T(8,128)S(1)}, f32[256,256]{1,0:T(8,128)}, u32[]{:S(2)}, u32[]{:S(2)}) collective-permute-start(f32[256,256]{1,0:T(8,128)S(1)} %get-tuple-element.718), channel_id=1, source_target_pairs={{1,0},{2,1},{3,2},{4,3},{5,4},{6,5},{7,6},{9,8},{10,9},{11,10},{12... | collective-permute-start | bytes 786440 | tf_op jit(solution)/shard_map/while/body/eval_jaxpr/ppermute | solution.py:13
  536.2 9.9 %collective-permute-start = (f32[256,256]{1,0:T(8,128)S(1)}, f32[256,256]{1,0:T(8,128)}, u32[]{:S(2)}, u32[]{:S(2)}) collective-permute-start(f32[256,256]{1,0:T(8,128)S(1)} %get-tuple-element.718), channel_id=1, source_target_pairs={{1,0},{2,1},{3,2},{4,3},{5,4},{6,5},{7,6},{9,8},{10,9},{11,10},{12... | collective-permute-start | bytes 786440 | tf_op jit(solution)/shard_map/while/body/eval_jaxpr/ppermute | solution.py:13
  555.8 9.9 %collective-permute-start = (f32[256,256]{1,0:T(8,128)S(1)}, f32[256,256]{1,0:T(8,128)}, u32[]{:S(2)}, u32[]{:S(2)}) collective-permute-start(f32[256,256]{1,0:T(8,128)S(1)} %get-tuple-element.718), channel_id=1, source_target_pairs={{1,0},{2,1},{3,2},{4,3},{5,4},{6,5},{7,6},{9,8},{10,9},{11,10},{12... | collective-permute-start | bytes 786440 | tf_op jit(solution)/shard_map/while/body/eval_jaxpr/ppermute | solution.py:13
  575.3 9.9 %collective-permute-start = (f32[256,256]{1,0:T(8,128)S(1)}, f32[256,256]{1,0:T(8,128)}, u32[]{:S(2)}, u32[]{:S(2)}) collective-permute-start(f32[256,256]{1,0:T(8,128)S(1)} %get-tuple-element.718), channel_id=1, source_target_pairs={{1,0},{2,1},{3,2},{4,3},{5,4},{6,5},{7,6},{9,8},{10,9},{11,10},{12... | collective-permute-start | bytes 786440 | tf_op jit(solution)/shard_map/while/body/eval_jaxpr/ppermute | solution.py:13
  587.3 20.5 %copy-start.2 = (s32[4,4,12]{2,1,0:T(4,128)S(1)}, s32[4,4,12]{2,1,0:T(4,128)}, u32[]{:S(2)}) copy-start(s32[4,4,12]{2,1,0:T(4,128)} %param.23) | copy-start | bytes 2308
  599.9 9.1 %collective-permute-start.2 = (f32[256,256]{1,0:T(8,128)S(1)}, f32[256,256]{1,0:T(8,128)S(1)}, u32[]{:S(2)}, u32[]{:S(2)}) collective-permute-start(f32[256,256]{1,0:T(8,128)S(1)} %get-tuple-element.504), channel_id=1, source_target_pairs={{0,1},{1,2},{2,3},{3,4},{4,5},{5,6},{6,7},{8,9},{9,10},{10,11},{11... | collective-permute-start | bytes 786440 | tf_op jit(solution)/shard_map/ppermute | solution.py:24
  605.6 12.8 %collective-permute-start.3 = (f32[256,256]{1,0:T(8,128)S(1)}, f32[256,256]{1,0:T(8,128)S(1)}, u32[]{:S(2)}, u32[]{:S(2)}) collective-permute-start(f32[256,256]{1,0:T(8,128)S(1)} %get-tuple-element.505), channel_id=1, source_target_pairs={{1,0},{2,1},{3,2},{4,3},{5,4},{6,5},{7,6},{9,8},{10,9},{11,10},{12... | collective-permute-start | bytes 786440 | tf_op jit(solution)/shard_map/ppermute | solution.py:26
  624.8 2.2 copy-start.1
Sparse Core Ops, SparseCore 0:
  9.8 134.8 all-gather.3
  146.4 152.9 all-gather.5
  301.2 158.2 all-gather.7
where the time goes:
time: 643 us; the launch traced here: 640 us
  waiting for transfers between devices  384 us (60%)
  matrix products  133 us (21%)
  starting transfers between devices  82.5 us (13%)
  local copies, waits for them, and re-layouts  17.9 us (3%)
  between operations  13.9 us (2%)
    all_gather x1, waiting for transfers between devices, on_device(): lax.all_gather(diag_inv, 'rhs', axis=1, tiled=True)  153 us
    all_gather x1, waiting for transfers between devices, on_device(): lax.all_gather(lower, 'rhs', axis=1, tiled=True)  131 us
    ppermute x14, waiting for transfers between devices, shifted(): lax.ppermute(value, axis, [(source, source + steps) for source in range(i...  88.2 us
    ppermute x14, starting transfers between devices, shifted(): lax.ppermute(value, axis, [(source, source + steps) for source in range(i...  74.5 us
    dot_general x32, matrix products, advance(): lax.dot_general(inv_block, forward_block - entering, TRANSPOSED, precisio...  52.3 us
    dot_general x32, matrix products, advance(): solved = jnp.dot(inv_block, rhs_block - coupled, precision=HIGHEST_PREC)  42.7 us
    dot_general x32, matrix products, advance(): lax.dot_general(low_block, solved, TRANSPOSED, precision=HIGHEST_PREC)  19.3 us
  transfers between devices with their start and end apart: 19, of which 18 were waited for; matrix products, arithmetic and copies ran while one was open for 22% of the time, Pallas kernels for 0%

commit v1 on v0

--- a/solution.py
+++ b/solution.py
@@ -84,7 +84,9 @@
     columns = right_side.shape[1]
     rhs_blocks = right_side.reshape(supers, panel_rows, columns)
     inverse, lower_all = (
-        lax.all_gather(diag_inv, "rhs", axis=1, tiled=True),
+        jnp.concatenate(
+            lax.all_to_all(jnp.stack([diag_inv] * lax.axis_size("rhs")), "rhs", 0, 0), axis=1
+        ),
         lax.all_gather(lower, "rhs", axis=1, tiled=True),
     )
     masked = apply_pattern(lower_all, factor_pattern)

time: 643 us -> 468 us (0.73)
  waiting for transfers between devices: 384 us -> 224 us
  matrix products: 133 us -> 106 us
  local copies, waits for them, and re-layouts: 17.9 us -> 26.5 us
    all_gather x1 -> x0, waiting for transfers between devices: 153 us -> none  [on_device(): lax.all_gather(diag_inv, 'rhs', axis=1, tiled=True)]
    dot_general x32, matrix products: 42.7 us -> 15.1 us  [advance(): solved = jnp.dot(inv_block, rhs_block - coupled, precision=HIGHEST_PREC)]
    all_gather x1, waiting for transfers between devices: 131 us -> 116 us  [on_device(): lax.all_gather(lower, 'rhs', axis=1, tiled=True)]
    all_to_all x0 -> x1, waiting for transfers between devices: none -> 12.3 us  [on_device(): lax.all_to_all(jnp.stack([diag_inv] * lax.axis_size('rhs')), 'rhs', 0, 0)]
    all_to_all x0 -> x1, starting transfers between devices: none -> 9.21 us  [on_device(): lax.all_to_all(jnp.stack([diag_inv] * lax.axis_size('rhs')), 'rhs', 0, 0)]
    while x14, local copies, waits for them, and re-layouts: 6.78 us -> 13.3 us
  transfers between devices with their start and end apart: 19 -> 19, of which waited for: 18 -> 18; matrix products, arithmetic and copies ran while one was open for 22% -> 27% of each run, Pallas kernels for 0% -> 0%
where the time goes in v1:
time: 468 us; the launch traced here: 466 us
  waiting for transfers between devices  224 us (48%)
  matrix products  106 us (23%)
  starting transfers between devices  88.7 us (19%)
  local copies, waits for them, and re-layouts  26.5 us (6%)
  between operations  14.2 us (3%)
  other arithmetic  5.41 us (1%)
    all_gather x1, waiting for transfers between devices, on_device(): lax.all_gather(lower, 'rhs', axis=1, tiled=True)  116 us
    ppermute x14, waiting for transfers between devices, shifted(): lax.ppermute(value, axis, [(source, source + steps) for source in range(i...  84.1 us
    ppermute x14, starting transfers between devices, shifted(): lax.ppermute(value, axis, [(source, source + steps) for source in range(i...  71.6 us
    dot_general x32, matrix products, advance(): lax.dot_general(inv_block, forward_block - entering, TRANSPOSED, precisio...  52.4 us
    dot_general x32, matrix products, advance(): lax.dot_general(low_block, solved, TRANSPOSED, precision=HIGHEST_PREC)  19.3 us
    dot_general x32, matrix products, advance(): solved = jnp.dot(inv_block, rhs_block - coupled, precision=HIGHEST_PREC)  15.1 us
    while x14, local copies, waits for them, and re-layouts  13.3 us
    all_to_all x1, waiting for transfers between devices, on_device(): lax.all_to_all(jnp.stack([diag_inv] * lax.axis_size('rhs')), 'rhs', 0, 0)  12.3 us
  transfers between devices with their start and end apart: 19, of which 18 were waited for; matrix products, arithmetic and copies ran while one was open for 27% of the time, Pallas kernels for 0%

profile of v1, /device:TPU:1, one launch (start us, length us, event | category | flops | bytes accessed | tf_op | source)
XLA Modules:
  0.0 466.0 jit_solution(3806899379153327105)
XLA Ops:
  9.8 9.2 %all-to-all-start = ((f32[32,4,8,256]{3,2,1,0:T(8,128)}), f32[32,4,8,256]{3,2,1,0:T(8,128)S(1)}, u32[]{:S(2)}, u32[]{:S(2)}) async-start(f32[32,4,8,256]{3,2,1,0:T(8,128)} %stack.2), calls=%async_computation | async-start | bytes 2097152 | tf_op jit(solution)/shard_map/all_to_all | solution.py:88
  22.2 12.3 %all-to-all-done = f32[32,4,8,256]{3,2,1,0:T(8,128)S(1)} async-done(((f32[32,4,8,256]{3,2,1,0:T(8,128)}), f32[32,4,8,256]{3,2,1,0:T(8,128)S(1)}, u32[]{:S(2)}, u32[]{:S(2)}) %all-to-all-start) | async-done | bytes 1048608 | tf_op jit(solution)/shard_map/all_to_all | solution.py:88
  34.6 116.2 %all-gather.3.cloned.1.call-done = f32[4,256,256]{2,1,0:T(8,128)} async-done(((f32[4,8,256]{2,1,0:T(8,128)}), f32[4,256,256]{2,1,0:T(8,128)}) %all-gather.3.cloned.1.call-update) | async-done | bytes 1048592 | tf_op jit(solution)/shard_map/all_gather | solution.py:90
  152.5 116.7 %while.89 = (s32[]{:T(128)}, f32[256,256]{1,0:T(8,128)S(1)}, f32[4,256,256]{2,1,0:T(8,128)S(1)}, f32[4,256,256]{2,1,0:T(8,128)S(1)}, f32[4,256,256]{2,1,0:T(8,12...) while((s32[]{:T(128)}, f32[256,256]{1,0:T(8,128)S(1)}, f32[4,256,256]{2,1,0:T(8,128)S(1)}, ...), condition=%wide.region_3.4_spmd, body=%wide.region_0.3_spmd.sunk | while | flops 402718720 | bytes 3409166 | solution.py:100
  152.6 3.2 while.94
  155.7 25.6 %collective-permute-start.1 = (f32[256,256]{1,0:T(8,128)S(1)}, f32[256,256]{1,0:T(8,128)}, u32[]{:S(2)}, u32[]{:S(2)}) collective-permute-start(f32[256,256]{1,0:T(8,128)S(1)} %get-tuple-element.703), channel_id=1, source_target_pairs={{0,1},{1,2},{2,3},{3,4},{4,5},{5,6},{6,7},{8,9},{9,10},{10,11},{11... | collective-permute-start | bytes 786440 | tf_op jit(solution)/shard_map/while/body/eval_jaxpr/ppermute | solution.py:13
  181.4 4.3 collective-permute-done.1
  186.7 3.2 while.94
  189.8 5.4 %collective-permute-start.1 = (f32[256,256]{1,0:T(8,128)S(1)}, f32[256,256]{1,0:T(8,128)}, u32[]{:S(2)}, u32[]{:S(2)}) collective-permute-start(f32[256,256]{1,0:T(8,128)S(1)} %get-tuple-element.703), channel_id=1, source_target_pairs={{0,1},{1,2},{2,3},{3,4},{4,5},{5,6},{6,7},{8,9},{9,10},{10,11},{11... | collective-permute-start | bytes 786440 | tf_op jit(solution)/shard_map/while/body/eval_jaxpr/ppermute | solution.py:13
  195.2 3.9 collective-permute-done.1
  200.1 3.2 while.94
  203.3 5.3 %collective-permute-start.1 = (f32[256,256]{1,0:T(8,128)S(1)}, f32[256,256]{1,0:T(8,128)}, u32[]{:S(2)}, u32[]{:S(2)}) collective-permute-start(f32[256,256]{1,0:T(8,128)S(1)} %get-tuple-element.703), channel_id=1, source_target_pairs={{0,1},{1,2},{2,3},{3,4},{4,5},{5,6},{6,7},{8,9},{9,10},{10,11},{11... | collective-permute-start | bytes 786440 | tf_op jit(solution)/shard_map/while/body/eval_jaxpr/ppermute | solution.py:13
  208.6 4.5 collective-permute-done.1
  214.1 3.2 while.94
  217.2 5.4 %collective-permute-start.1 = (f32[256,256]{1,0:T(8,128)S(1)}, f32[256,256]{1,0:T(8,128)}, u32[]{:S(2)}, u32[]{:S(2)}) collective-permute-start(f32[256,256]{1,0:T(8,128)S(1)} %get-tuple-element.703), channel_id=1, source_target_pairs={{0,1},{1,2},{2,3},{3,4},{4,5},{5,6},{6,7},{8,9},{9,10},{10,11},{11... | collective-permute-start | bytes 786440 | tf_op jit(solution)/shard_map/while/body/eval_jaxpr/ppermute | solution.py:13
  222.6 4.8 %collective-permute-done.1 = f32[256,256]{1,0:T(8,128)} collective-permute-done((f32[256,256]{1,0:T(8,128)S(1)}, f32[256,256]{1,0:T(8,128)}, u32[]{:S(2)}, u32[]{:S(2)}) %collective-permute-start.1) | collective-permute-done | bytes 262176 | tf_op jit(solution)/shard_map/while/body/eval_jaxpr/ppermute | solution.py:13
  228.3 3.2 while.94
  231.5 5.4 %collective-permute-start.1 = (f32[256,256]{1,0:T(8,128)S(1)}, f32[256,256]{1,0:T(8,128)}, u32[]{:S(2)}, u32[]{:S(2)}) collective-permute-start(f32[256,256]{1,0:T(8,128)S(1)} %get-tuple-element.703), channel_id=1, source_target_pairs={{0,1},{1,2},{2,3},{3,4},{4,5},{5,6},{6,7},{8,9},{9,10},{10,11},{11... | collective-permute-start | bytes 786440 | tf_op jit(solution)/shard_map/while/body/eval_jaxpr/ppermute | solution.py:13
  236.9 3.6 collective-permute-done.1
  241.4 3.2 while.94
  244.6 5.4 %collective-permute-start.1 = (f32[256,256]{1,0:T(8,128)S(1)}, f32[256,256]{1,0:T(8,128)}, u32[]{:S(2)}, u32[]{:S(2)}) collective-permute-start(f32[256,256]{1,0:T(8,128)S(1)} %get-tuple-element.703), channel_id=1, source_target_pairs={{0,1},{1,2},{2,3},{3,4},{4,5},{5,6},{6,7},{8,9},{9,10},{10,11},{11... | collective-permute-start | bytes 786440 | tf_op jit(solution)/shard_map/while/body/eval_jaxpr/ppermute | solution.py:13
  250.0 4.5 collective-permute-done.1
  255.5 3.2 while.94
  258.6 5.5 %collective-permute-start.1 = (f32[256,256]{1,0:T(8,128)S(1)}, f32[256,256]{1,0:T(8,128)}, u32[]{:S(2)}, u32[]{:S(2)}) collective-permute-start(f32[256,256]{1,0:T(8,128)S(1)} %get-tuple-element.703), channel_id=1, source_target_pairs={{0,1},{1,2},{2,3},{3,4},{4,5},{5,6},{6,7},{8,9},{9,10},{10,11},{11... | collective-permute-start | bytes 786440 | tf_op jit(solution)/shard_map/while/body/eval_jaxpr/ppermute | solution.py:13
  264.2 4.1 collective-permute-done.1
  270.3 5.9 %while.90 = (s32[]{:T(128)}, f32[256,256]{1,0:T(8,128)S(1)}, f32[4,256,256]{2,1,0:T(8,128)}, f32[4,256,256]{2,1,0:T(8,128)S(1)}, f32[4,256,256]{2,1,0:T(8,128)S(1)}, /*index=5*/f32[4,256,256]{2,1,0:T(8,128)S(1)}, s32[]{:T(128)}) while((s32[]{:T(128)}, f32[256,256]{1,0:T(8,128)S(1)}, f32[4,256,256]{2,1,0:T(8,128)}, ...), condition=%wide.region_5.6_spmd, body=%wide.region_4.5_spmd.sunk | while | flops 402718720 | bytes 2099285 | solution.py:49
  276.2 135.7 %while.92 = (s32[]{:T(128)}, f32[256,256]{1,0:T(8,128)S(1)}, f32[4,256,256]{2,1,0:T(8,128)S(1)}, f32[4,256,256]{2,1,0:T(8,128)S(1)}, f32[4,256,256]{2,1,0:T(8,12...) while((s32[]{:T(128)}, f32[256,256]{1,0:T(8,128)S(1)}, f32[4,256,256]{2,1,0:T(8,128)S(1)}, ...), condition=%wide.region_9.10_spmd, body=%wide.region_6.9_spmd.sunk | while | flops 402718720 | bytes 3409194 | solution.py:107
  276.2 8.7 %while.95 = (s32[]{:T(128)}, f32[256,256]{1,0:T(8,128)S(1)}, f32[4,256,256]{2,1,0:T(8,128)S(1)}, f32[4,256,256]{2,1,0:T(8,128)S(1)}, f32[4,256,256]{2,1,0:T(8,128)}, /*index=5*/s32[]{:T(128)}, s32[]{:T(128)}) while((s32[]{:T(128)}, f32[256,256]{1,0:T(8,128)S(1)}, f32[4,256,256]{2,1,0:T(8,128)S(1)}, f32[4,256,256]{2,1,0:T(8,128)S(1)}, ...), condition=%wide.region_8.8_spmd, body=%wide.region_7.7_spmd.sunk | while | flops 402718720 | bytes 1836133 | solution.py:63
  286.9 8.0 %collective-permute-done = f32[256,256]{1,0:T(8,128)} collective-permute-done((f32[256,256]{1,0:T(8,128)S(1)}, f32[256,256]{1,0:T(8,128)}, u32[]{:S(2)}, u32[]{:S(2)}) %collective-permute-start) | collective-permute-done | bytes 262176 | tf_op jit(solution)/shard_map/while/body/eval_jaxpr/ppermute | solution.py:13
  295.8 8.7 %while.95 = (s32[]{:T(128)}, f32[256,256]{1,0:T(8,128)S(1)}, f32[4,256,256]{2,1,0:T(8,128)S(1)}, f32[4,256,256]{2,1,0:T(8,128)S(1)}, f32[4,256,256]{2,1,0:T(8,128)}, /*index=5*/s32[]{:T(128)}, s32[]{:T(128)}) while((s32[]{:T(128)}, f32[256,256]{1,0:T(8,128)S(1)}, f32[4,256,256]{2,1,0:T(8,128)S(1)}, f32[4,256,256]{2,1,0:T(8,128)S(1)}, ...), condition=%wide.region_8.8_spmd, body=%wide.region_7.7_spmd.sunk | while | flops 402718720 | bytes 1836133 | solution.py:63
  306.5 7.1 %collective-permute-done = f32[256,256]{1,0:T(8,128)} collective-permute-done((f32[256,256]{1,0:T(8,128)S(1)}, f32[256,256]{1,0:T(8,128)}, u32[]{:S(2)}, u32[]{:S(2)}) %collective-permute-start) | collective-permute-done | bytes 262176 | tf_op jit(solution)/shard_map/while/body/eval_jaxpr/ppermute | solution.py:13
  314.5 8.7 %while.95 = (s32[]{:T(128)}, f32[256,256]{1,0:T(8,128)S(1)}, f32[4,256,256]{2,1,0:T(8,128)S(1)}, f32[4,256,256]{2,1,0:T(8,128)S(1)}, f32[4,256,256]{2,1,0:T(8,128)}, /*index=5*/s32[]{:T(128)}, s32[]{:T(128)}) while((s32[]{:T(128)}, f32[256,256]{1,0:T(8,128)S(1)}, f32[4,256,256]{2,1,0:T(8,128)S(1)}, f32[4,256,256]{2,1,0:T(8,128)S(1)}, ...), condition=%wide.region_8.8_spmd, body=%wide.region_7.7_spmd.sunk | while | flops 402718720 | bytes 1836133 | solution.py:63
  325.2 6.8 %collective-permute-done = f32[256,256]{1,0:T(8,128)} collective-permute-done((f32[256,256]{1,0:T(8,128)S(1)}, f32[256,256]{1,0:T(8,128)}, u32[]{:S(2)}, u32[]{:S(2)}) %collective-permute-start) | collective-permute-done | bytes 262176 | tf_op jit(solution)/shard_map/while/body/eval_jaxpr/ppermute | solution.py:13
  332.9 8.7 %while.95 = (s32[]{:T(128)}, f32[256,256]{1,0:T(8,128)S(1)}, f32[4,256,256]{2,1,0:T(8,128)S(1)}, f32[4,256,256]{2,1,0:T(8,128)S(1)}, f32[4,256,256]{2,1,0:T(8,128)}, /*index=5*/s32[]{:T(128)}, s32[]{:T(128)}) while((s32[]{:T(128)}, f32[256,256]{1,0:T(8,128)S(1)}, f32[4,256,256]{2,1,0:T(8,128)S(1)}, f32[4,256,256]{2,1,0:T(8,128)S(1)}, ...), condition=%wide.region_8.8_spmd, body=%wide.region_7.7_spmd.sunk | while | flops 402718720 | bytes 1836133 | solution.py:63
  343.6 8.3 %collective-permute-done = f32[256,256]{1,0:T(8,128)} collective-permute-done((f32[256,256]{1,0:T(8,128)S(1)}, f32[256,256]{1,0:T(8,128)}, u32[]{:S(2)}, u32[]{:S(2)}) %collective-permute-start) | collective-permute-done | bytes 262176 | tf_op jit(solution)/shard_map/while/body/eval_jaxpr/ppermute | solution.py:13
  352.8 8.7 %while.95 = (s32[]{:T(128)}, f32[256,256]{1,0:T(8,128)S(1)}, f32[4,256,256]{2,1,0:T(8,128)S(1)}, f32[4,256,256]{2,1,0:T(8,128)S(1)}, f32[4,256,256]{2,1,0:T(8,128)}, /*index=5*/s32[]{:T(128)}, s32[]{:T(128)}) while((s32[]{:T(128)}, f32[256,256]{1,0:T(8,128)S(1)}, f32[4,256,256]{2,1,0:T(8,128)S(1)}, f32[4,256,256]{2,1,0:T(8,128)S(1)}, ...), condition=%wide.region_8.8_spmd, body=%wide.region_7.7_spmd.sunk | while | flops 402718720 | bytes 1836133 | solution.py:63
  363.4 8.3 %collective-permute-done = f32[256,256]{1,0:T(8,128)} collective-permute-done((f32[256,256]{1,0:T(8,128)S(1)}, f32[256,256]{1,0:T(8,128)}, u32[]{:S(2)}, u32[]{:S(2)}) %collective-permute-start) | collective-permute-done | bytes 262176 | tf_op jit(solution)/shard_map/while/body/eval_jaxpr/ppermute | solution.py:13
  372.7 8.7 %while.95 = (s32[]{:T(128)}, f32[256,256]{1,0:T(8,128)S(1)}, f32[4,256,256]{2,1,0:T(8,128)S(1)}, f32[4,256,256]{2,1,0:T(8,128)S(1)}, f32[4,256,256]{2,1,0:T(8,128)}, /*index=5*/s32[]{:T(128)}, s32[]{:T(128)}) while((s32[]{:T(128)}, f32[256,256]{1,0:T(8,128)S(1)}, f32[4,256,256]{2,1,0:T(8,128)S(1)}, f32[4,256,256]{2,1,0:T(8,128)S(1)}, ...), condition=%wide.region_8.8_spmd, body=%wide.region_7.7_spmd.sunk | while | flops 402718720 | bytes 1836133 | solution.py:63
  383.3 8.1 %collective-permute-done = f32[256,256]{1,0:T(8,128)} collective-permute-done((f32[256,256]{1,0:T(8,128)S(1)}, f32[256,256]{1,0:T(8,128)}, u32[]{:S(2)}, u32[]{:S(2)}) %collective-permute-start) | collective-permute-done | bytes 262176 | tf_op jit(solution)/shard_map/while/body/eval_jaxpr/ppermute | solution.py:13
  392.4 8.7 %while.95 = (s32[]{:T(128)}, f32[256,256]{1,0:T(8,128)S(1)}, f32[4,256,256]{2,1,0:T(8,128)S(1)}, f32[4,256,256]{2,1,0:T(8,128)S(1)}, f32[4,256,256]{2,1,0:T(8,128)}, /*index=5*/s32[]{:T(128)}, s32[]{:T(128)}) while((s32[]{:T(128)}, f32[256,256]{1,0:T(8,128)S(1)}, f32[4,256,256]{2,1,0:T(8,128)S(1)}, f32[4,256,256]{2,1,0:T(8,128)S(1)}, ...), condition=%wide.region_8.8_spmd, body=%wide.region_7.7_spmd.sunk | while | flops 402718720 | bytes 1836133 | solution.py:63
  403.0 8.0 %collective-permute-done = f32[256,256]{1,0:T(8,128)} collective-permute-done((f32[256,256]{1,0:T(8,128)S(1)}, f32[256,256]{1,0:T(8,128)}, u32[]{:S(2)}, u32[]{:S(2)}) %collective-permute-start) | collective-permute-done | bytes 262176 | tf_op jit(solution)/shard_map/while/body/eval_jaxpr/ppermute | solution.py:13
  413.0 11.5 %while.93 = (s32[]{:T(128)}, f32[256,256]{1,0:T(8,128)S(1)}, f32[4,256,256]{2,1,0:T(8,128)}, f32[4,256,256]{2,1,0:T(8,128)S(1)}, f32[4,256,256]{2,1,0:T(8,128)S(...) while((s32[]{:T(128)}, f32[256,256]{1,0:T(8,128)S(1)}, f32[4,256,256]{2,1,0:T(8,128)}, ...), condition=%wide.region_11.12_spmd, body=%wide.region_10.11_spmd.sunk | while | flops 402718720 | bytes 2098797 | solution.py:63
  413.0 2.3 bitcast_dynamic-update-slice_fusion.5
  415.9 2.3 bitcast_dynamic-update-slice_fusion.5
  425.6 5.7 %collective-permute-start.2 = (f32[256,256]{1,0:T(8,128)S(1)}, f32[256,256]{1,0:T(8,128)S(1)}, u32[]{:S(2)}, u32[]{:S(2)}) collective-permute-start(f32[256,256]{1,0:T(8,128)S(1)} %get-tuple-element.504), channel_id=1, source_target_pairs={{0,1},{1,2},{2,3},{3,4},{4,5},{5,6},{6,7},{8,9},{9,10},{10,11},{11... | collective-permute-start | bytes 786440 | tf_op jit(solution)/shard_map/ppermute | solution.py:24
  434.7 9.5 %collective-permute-done.3 = f32[256,256]{1,0:T(8,128)S(1)} collective-permute-done((f32[256,256]{1,0:T(8,128)S(1)}, f32[256,256]{1,0:T(8,128)S(1)}, u32[]{:S(2)}, u32[]{:S(2)}) %collective-permute-start.3) | collective-permute-done | bytes 262176 | tf_op jit(solution)/shard_map/ppermute | solution.py:26
  445.7 4.9 %copy.16 = f32[4,256,768]{1,2,0:T(8,128)} copy(f32[4,256,768]{2,0,1:T(4,128)} %all-gather.5.cloned.1.call-done) | data formatting | bytes 6291456 | tf_op jit(solution)/shard_map/all_gather | solution.py:116
  452.8 6.4 %fusion.38 = f32[4,256,256]{2,1,0:T(8,128)} fusion(f32[4,256,256]{2,1,0:T(8,128)S(1)} %get-tuple-element.897, f32[4,256,768]{1,2,0:T(8,128)S(1)} %bitcast_multiply_fusion, f32[4,256,256]{2,1,0:T(8,128)S(1)} %bitcast.117, f32[4,256,256]{2,1,0:T(8,128)S(1)} %copy-done.1, f32[4,256,256]{2,1,0:T(8,128)S(1)} %bitcast.116), kind=kOutput, calls=%fused_computation.45 | convolution fusion | flops 2417754112 | bytes 8388608 | tf_op jit(solution)/shard_map/sij,sjr->sir/dot_general | solution.py:78
  (180 shorter events, 139.0 us)
Async XLA Ops:
  7.2 11.9 %copy-start.2 = (f32[4,8,768]{2,1,0:T(8,128)S(1)}, f32[4,8,768]{2,1,0:T(8,128)}, u32[]{:S(2)}) copy-start(f32[4,8,768]{2,1,0:T(8,128)} %param.22) | copy-start | bytes 294916
  7.2 12.6 %copy-start.4 = (s32[4,4,4]{2,1,0:T(4,128)S(1)}, s32[4,4,4]{2,1,0:T(4,128)}, u32[]{:S(2)}) copy-start(s32[4,4,4]{2,1,0:T(4,128)} %param.21) | copy-start | bytes 772
  7.2 143.6 %all-gather.3.cloned.1.call-start = ((), (), s32[]{:S(2)}) async-start(), calls=%async_computation.1 | async-start | bytes 1081344 | tf_op jit(solution)/shard_map/all_gather | solution.py:90
  9.8 24.7 %all-to-all-start = ((f32[32,4,8,256]{3,2,1,0:T(8,128)}), f32[32,4,8,256]{3,2,1,0:T(8,128)S(1)}, u32[]{:S(2)}, u32[]{:S(2)}) async-start(f32[32,4,8,256]{3,2,1,0:T(8,128)} %stack.2), calls=%async_computation | async-start | bytes 2097152 | tf_op jit(solution)/shard_map/all_to_all | solution.py:88
  19.0 426.7 %all-gather.5.cloned.1.call-start = ((), (), s32[]{:S(2)}) async-start(), calls=%async_computation.2 | async-start | bytes 3244032 | tf_op jit(solution)/shard_map/all_gather | solution.py:116
  22.2 130.3 %copy-start = (f32[1024,256]{1,0:T(8,128)S(1)}, f32[1024,256]{1,0:T(8,128)}, u32[]{:S(2)}) copy-start(f32[1024,256]{1,0:T(8,128)} %param.18) | copy-start | bytes 3145732
  155.7 30.0 %collective-permute-start.1 = (f32[256,256]{1,0:T(8,128)S(1)}, f32[256,256]{1,0:T(8,128)}, u32[]{:S(2)}, u32[]{:S(2)}) collective-permute-start(f32[256,256]{1,0:T(8,128)S(1)} %get-tuple-element.703), channel_id=1, source_target_pairs={{0,1},{1,2},{2,3},{3,4},{4,5},{5,6},{6,7},{8,9},{9,10},{10,11},{11... | collective-permute-start | bytes 786440 | tf_op jit(solution)/shard_map/while/body/eval_jaxpr/ppermute | solution.py:13
  189.8 9.3 %collective-permute-start.1 = (f32[256,256]{1,0:T(8,128)S(1)}, f32[256,256]{1,0:T(8,128)}, u32[]{:S(2)}, u32[]{:S(2)}) collective-permute-start(f32[256,256]{1,0:T(8,128)S(1)} %get-tuple-element.703), channel_id=1, source_target_pairs={{0,1},{1,2},{2,3},{3,4},{4,5},{5,6},{6,7},{8,9},{9,10},{10,11},{11... | collective-permute-start | bytes 786440 | tf_op jit(solution)/shard_map/while/body/eval_jaxpr/ppermute | solution.py:13
  203.3 9.9 %collective-permute-start.1 = (f32[256,256]{1,0:T(8,128)S(1)}, f32[256,256]{1,0:T(8,128)}, u32[]{:S(2)}, u32[]{:S(2)}) collective-permute-start(f32[256,256]{1,0:T(8,128)S(1)} %get-tuple-element.703), channel_id=1, source_target_pairs={{0,1},{1,2},{2,3},{3,4},{4,5},{5,6},{6,7},{8,9},{9,10},{10,11},{11... | collective-permute-start | bytes 786440 | tf_op jit(solution)/shard_map/while/body/eval_jaxpr/ppermute | solution.py:13
  217.2 10.1 %collective-permute-start.1 = (f32[256,256]{1,0:T(8,128)S(1)}, f32[256,256]{1,0:T(8,128)}, u32[]{:S(2)}, u32[]{:S(2)}) collective-permute-start(f32[256,256]{1,0:T(8,128)S(1)} %get-tuple-element.703), channel_id=1, source_target_pairs={{0,1},{1,2},{2,3},{3,4},{4,5},{5,6},{6,7},{8,9},{9,10},{10,11},{11... | collective-permute-start | bytes 786440 | tf_op jit(solution)/shard_map/while/body/eval_jaxpr/ppermute | solution.py:13
  231.5 9.0 %collective-permute-start.1 = (f32[256,256]{1,0:T(8,128)S(1)}, f32[256,256]{1,0:T(8,128)}, u32[]{:S(2)}, u32[]{:S(2)}) collective-permute-start(f32[256,256]{1,0:T(8,128)S(1)} %get-tuple-element.703), channel_id=1, source_target_pairs={{0,1},{1,2},{2,3},{3,4},{4,5},{5,6},{6,7},{8,9},{9,10},{10,11},{11... | collective-permute-start | bytes 786440 | tf_op jit(solution)/shard_map/while/body/eval_jaxpr/ppermute | solution.py:13
  244.6 10.0 %collective-permute-start.1 = (f32[256,256]{1,0:T(8,128)S(1)}, f32[256,256]{1,0:T(8,128)}, u32[]{:S(2)}, u32[]{:S(2)}) collective-permute-start(f32[256,256]{1,0:T(8,128)S(1)} %get-tuple-element.703), channel_id=1, source_target_pairs={{0,1},{1,2},{2,3},{3,4},{4,5},{5,6},{6,7},{8,9},{9,10},{10,11},{11... | collective-permute-start | bytes 786440 | tf_op jit(solution)/shard_map/while/body/eval_jaxpr/ppermute | solution.py:13
  258.6 9.6 %collective-permute-start.1 = (f32[256,256]{1,0:T(8,128)S(1)}, f32[256,256]{1,0:T(8,128)}, u32[]{:S(2)}, u32[]{:S(2)}) collective-permute-start(f32[256,256]{1,0:T(8,128)S(1)} %get-tuple-element.703), channel_id=1, source_target_pairs={{0,1},{1,2},{2,3},{3,4},{4,5},{5,6},{6,7},{8,9},{9,10},{10,11},{11... | collective-permute-start | bytes 786440 | tf_op jit(solution)/shard_map/while/body/eval_jaxpr/ppermute | solution.py:13
  285.0 9.9 %collective-permute-start = (f32[256,256]{1,0:T(8,128)S(1)}, f32[256,256]{1,0:T(8,128)}, u32[]{:S(2)}, u32[]{:S(2)}) collective-permute-start(f32[256,256]{1,0:T(8,128)S(1)} %get-tuple-element.718), channel_id=1, source_target_pairs={{1,0},{2,1},{3,2},{4,3},{5,4},{6,5},{7,6},{9,8},{10,9},{11,10},{12... | collective-permute-start | bytes 786440 | tf_op jit(solution)/shard_map/while/body/eval_jaxpr/ppermute | solution.py:13
  304.5 9.0 %collective-permute-start = (f32[256,256]{1,0:T(8,128)S(1)}, f32[256,256]{1,0:T(8,128)}, u32[]{:S(2)}, u32[]{:S(2)}) collective-permute-start(f32[256,256]{1,0:T(8,128)S(1)} %get-tuple-element.718), channel_id=1, source_target_pairs={{1,0},{2,1},{3,2},{4,3},{5,4},{6,5},{7,6},{9,8},{10,9},{11,10},{12... | collective-permute-start | bytes 786440 | tf_op jit(solution)/shard_map/while/body/eval_jaxpr/ppermute | solution.py:13
  323.3 8.7 %collective-permute-start = (f32[256,256]{1,0:T(8,128)S(1)}, f32[256,256]{1,0:T(8,128)}, u32[]{:S(2)}, u32[]{:S(2)}) collective-permute-start(f32[256,256]{1,0:T(8,128)S(1)} %get-tuple-element.718), channel_id=1, source_target_pairs={{1,0},{2,1},{3,2},{4,3},{5,4},{6,5},{7,6},{9,8},{10,9},{11,10},{12... | collective-permute-start | bytes 786440 | tf_op jit(solution)/shard_map/while/body/eval_jaxpr/ppermute | solution.py:13
  341.6 10.2 %collective-permute-start = (f32[256,256]{1,0:T(8,128)S(1)}, f32[256,256]{1,0:T(8,128)}, u32[]{:S(2)}, u32[]{:S(2)}) collective-permute-start(f32[256,256]{1,0:T(8,128)S(1)} %get-tuple-element.718), channel_id=1, source_target_pairs={{1,0},{2,1},{3,2},{4,3},{5,4},{6,5},{7,6},{9,8},{10,9},{11,10},{12... | collective-permute-start | bytes 786440 | tf_op jit(solution)/shard_map/while/body/eval_jaxpr/ppermute | solution.py:13
  361.5 10.2 %collective-permute-start = (f32[256,256]{1,0:T(8,128)S(1)}, f32[256,256]{1,0:T(8,128)}, u32[]{:S(2)}, u32[]{:S(2)}) collective-permute-start(f32[256,256]{1,0:T(8,128)S(1)} %get-tuple-element.718), channel_id=1, source_target_pairs={{1,0},{2,1},{3,2},{4,3},{5,4},{6,5},{7,6},{9,8},{10,9},{11,10},{12... | collective-permute-start | bytes 786440 | tf_op jit(solution)/shard_map/while/body/eval_jaxpr/ppermute | solution.py:13
  381.4 10.0 %collective-permute-start = (f32[256,256]{1,0:T(8,128)S(1)}, f32[256,256]{1,0:T(8,128)}, u32[]{:S(2)}, u32[]{:S(2)}) collective-permute-start(f32[256,256]{1,0:T(8,128)S(1)} %get-tuple-element.718), channel_id=1, source_target_pairs={{1,0},{2,1},{3,2},{4,3},{5,4},{6,5},{7,6},{9,8},{10,9},{11,10},{12... | collective-permute-start | bytes 786440 | tf_op jit(solution)/shard_map/while/body/eval_jaxpr/ppermute | solution.py:13
  401.1 9.9 %collective-permute-start = (f32[256,256]{1,0:T(8,128)S(1)}, f32[256,256]{1,0:T(8,128)}, u32[]{:S(2)}, u32[]{:S(2)}) collective-permute-start(f32[256,256]{1,0:T(8,128)S(1)} %get-tuple-element.718), channel_id=1, source_target_pairs={{1,0},{2,1},{3,2},{4,3},{5,4},{6,5},{7,6},{9,8},{10,9},{11,10},{12... | collective-permute-start | bytes 786440 | tf_op jit(solution)/shard_map/while/body/eval_jaxpr/ppermute | solution.py:13
  413.0 20.5 %copy-start.3 = (s32[4,4,12]{2,1,0:T(4,128)S(1)}, s32[4,4,12]{2,1,0:T(4,128)}, u32[]{:S(2)}) copy-start(s32[4,4,12]{2,1,0:T(4,128)} %param.23) | copy-start | bytes 2308
  425.6 9.0 %collective-permute-start.2 = (f32[256,256]{1,0:T(8,128)S(1)}, f32[256,256]{1,0:T(8,128)S(1)}, u32[]{:S(2)}, u32[]{:S(2)}) collective-permute-start(f32[256,256]{1,0:T(8,128)S(1)} %get-tuple-element.504), channel_id=1, source_target_pairs={{0,1},{1,2},{2,3},{3,4},{4,5},{5,6},{6,7},{8,9},{9,10},{10,11},{11... | collective-permute-start | bytes 786440 | tf_op jit(solution)/shard_map/ppermute | solution.py:24
  431.4 12.8 %collective-permute-start.3 = (f32[256,256]{1,0:T(8,128)S(1)}, f32[256,256]{1,0:T(8,128)S(1)}, u32[]{:S(2)}, u32[]{:S(2)}) collective-permute-start(f32[256,256]{1,0:T(8,128)S(1)} %get-tuple-element.505), channel_id=1, source_target_pairs={{1,0},{2,1},{3,2},{4,3},{5,4},{6,5},{7,6},{9,8},{10,9},{11,10},{12... | collective-permute-start | bytes 786440 | tf_op jit(solution)/shard_map/ppermute | solution.py:26
  450.6 2.2 copy-start.1
Sparse Core Ops, SparseCore 0:
  9.8 140.9 all-gather.2
  152.6 156.0 all-gather.4
